TPU v7x, 32 devices: a whole 2x2x4 slice. The times are simulated.
32 devices in a mesh: groups: 2 (over x), blk: 16 (over z, y, core).
Axes of the slice: x: 2, y: 2, z: 4, core: 2. Of those that a mesh axis runs over, the one named last changes fastest.
Arguments:
- hidden: bfloat16 [16384, 2048], P(('groups', 'blk')), parts along dimension 0, may hold values from -6 to 6
- kept_idx: int32 [32, 128], P(('groups', 'blk')), parts along dimension 0, may hold values from 0 to 511, as said below
- kept_count: int32 [32], P(('groups', 'blk')), parts along dimension 0, may hold values from 0 to 128, as said below
- router: bfloat16 [2048], replicated, may hold values from -0.125 to 0.125
- norm_gain: float32 [2048], replicated, may hold values from 0.25 to 1.75
- qk_gain: float32 [2, 64], replicated, may hold values from 1 to 7
- query_weight: bfloat16 [2048, 2048], P('blk'), may hold values from -1 to 1
- key_weight: bfloat16 [2048, 128], P('blk'), may hold values from -1 to 1
- value_weight: bfloat16 [2048, 128], P('blk'), may hold values from -0.125 to 0.125
- out_weight: bfloat16 [2048, 2048], P('blk'), may hold values from -0.375 to 0.375
Outputs:
- mixed: bfloat16 [16384, 2048], P(('groups', 'blk')), parts along dimension 0
There are 2 independent parts, one for each index of `groups`. A program takes and returns all parts, laid end to end along the dimension named above; an argument that names none is the same for every part. Nothing has to cross between parts.
Inputs may be any that keep to these rules, and one draw needn't show every extreme that they name: `kept_count`: the counts sum to 1024; in every draw some shard's count is exactly 128. `kept_idx`: in row s the first kept_count[s] entries are distinct local token indices in increasing order; entries past the count are 0.
All inputs are finite; a program needn't handle non-finite values.
Results may differ from a plain program's by a relative error of at most 0.01.
Values may be sent and summed in bfloat16 or wider, within the bound.
A program may use at most 128 MiB of HBM per device.

v0:
```python
import math
import jax
import jax.numpy as jnp
from jax import lax
from jax.sharding import PartitionSpec as P

Q_HEADS = 32
KV_HEADS = 2
HEAD = 64
TOK_DEV = 512
KEEP_DEV = 64
CAP = 128
norm_eps = 1e-06
rope_base = 1000000.0


def rms_scale(values, scales):
    return values * lax.rsqrt(jnp.mean(values * values, axis=-1, keepdims=True) + norm_eps) * scales


def rotate(values, angles):
    half_size = values.shape[-1] // 2
    lower_half = values[..., :half_size]
    upper_half = values[..., half_size:]
    cosine = jnp.cos(angles)
    sine_part = jnp.sin(angles)
    return jnp.concatenate(
        [
            lower_half * cosine - upper_half * sine_part,
            upper_half * cosine + lower_half * sine_part,
        ],
        axis=-1,
    )


def attend(query_heads, query_ranks, key_block, value_block, key_ranks, state):
    prev_top, prev_total, prev_acc = state
    length = key_block.shape[0]
    keys_split = key_block.reshape(length, KV_HEADS, HEAD)
    values_split = value_block.reshape(length, KV_HEADS, HEAD)
    scores = jnp.einsum(
        "agch,bgh->gcab", query_heads, keys_split, preferred_element_type=jnp.float32
    ) * (1.0 / math.sqrt(HEAD))
    allowed = key_ranks[None, :] <= query_ranks[:, None]
    masked = jnp.where(allowed, scores, -1e30)
    new_top = jnp.maximum(prev_top, jnp.max(masked, axis=-1))
    weights = jnp.where(allowed, jnp.exp(masked - new_top[..., None]), 0.0)
    factor = jnp.exp(prev_top - new_top)
    new_total = prev_total * factor + jnp.sum(weights, axis=-1)
    new_acc = prev_acc * factor[..., None] + jnp.einsum(
        "gcab,bgh->gcah",
        weights.astype(jnp.bfloat16),
        values_split,
        preferred_element_type=jnp.float32,
    )
    return (new_top, new_total, new_acc)


def make_fold(query_heads, query_ranks, rank_of, state, pieces):
    key_piece, value_piece = pieces
    length = key_piece.shape[0]

    def inner(block_turn, inner_state):
        block_start = block_turn * 512
        key_block = lax.dynamic_slice_in_dim(key_piece, block_start, 512, 0)
        value_block = lax.dynamic_slice_in_dim(value_piece, block_start, 512, 0)
        key_ranks = rank_of(block_start + jnp.arange(512, dtype=jnp.int32))
        return attend(query_heads, query_ranks, key_block, value_block, key_ranks, inner_state)

    return lax.fori_loop(0, length // 512, inner, state)


def body(
    hidden,
    kept_idx,
    kept_count,
    router,
    norm_gain,
    qk_gain,
    query_weight,
    key_weight,
    value_weight,
    out_weight,
):
    shard_count = lax.axis_size("blk")
    device = lax.axis_index("blk")
    width = hidden.shape[1]
    all_lists, all_counts = (
        lax.all_gather(kept_idx, "blk", axis=0, tiled=True),
        lax.all_gather(kept_count, "blk", axis=0, tiled=True),
    )
    starts = jnp.cumsum(all_counts) - all_counts
    own_start = starts[device]
    own_count = all_counts[device]
    list_slots = jnp.arange(CAP, dtype=jnp.int32)
    is_valid = list_slots < own_count
    token_rows = hidden[kept_idx[0]]
    gate_value = jax.nn.sigmoid(jnp.dot(token_rows, router, preferred_element_type=jnp.float32))
    slot_count = (CAP + shard_count - 1) // shard_count
    outgoing = jnp.where(is_valid[:, None], token_rows, jnp.zeros_like(token_rows))
    outgoing = jnp.roll(outgoing.reshape(slot_count, shard_count, width), own_start, axis=1)
    incoming = lax.all_to_all(outgoing, "blk", split_axis=1, concat_axis=1, tiled=True)
    query_ranks = device + jnp.arange(KEEP_DEV, dtype=jnp.int32) * shard_count
    source_ends = starts + all_counts
    source = jnp.sum((source_ends[None, :] <= query_ranks[:, None]).astype(jnp.int32), axis=1)
    within = query_ranks - starts[source]
    flat_index = within // shard_count * shard_count + source
    kept_rows = incoming.reshape(slot_count * shard_count, width)[flat_index]
    positions = source * TOK_DEV + all_lists[source, within]
    row_total = kept_rows.shape[0]
    normed = rms_scale(kept_rows.astype(jnp.float32), norm_gain).astype(jnp.bfloat16)
    query_cols = Q_HEADS * HEAD
    kv_cols = KV_HEADS * HEAD
    full_query, full_key, full_value, full_out = (
        lax.all_gather(query_weight, "blk", axis=0, tiled=True),
        lax.all_gather(key_weight, "blk", axis=0, tiled=True),
        lax.all_gather(value_weight, "blk", axis=0, tiled=True),
        lax.all_gather(out_weight, "blk", axis=0, tiled=True),
    )
    query_lin = jnp.dot(normed, full_query, preferred_element_type=jnp.float32)
    key_lin = jnp.dot(normed, full_key, preferred_element_type=jnp.float32)
    value_lin = jnp.dot(normed, full_value, preferred_element_type=jnp.float32)
    half_size = HEAD // 2
    rotation_rates = rope_base ** (-(jnp.arange(half_size, dtype=jnp.float32) * 2.0 / HEAD))
    angles = (positions.astype(jnp.float32)[:, None] * rotation_rates[None, :])[:, None, :]
    query_heads = rotate(
        rms_scale(query_lin.reshape(row_total, Q_HEADS, HEAD), qk_gain[0]), angles
    ).astype(jnp.bfloat16)
    key_heads = rotate(
        rms_scale(key_lin.reshape(row_total, KV_HEADS, HEAD), qk_gain[1]), angles
    ).astype(jnp.bfloat16)
    query_heads = query_heads.reshape(row_total, KV_HEADS, Q_HEADS // KV_HEADS, HEAD)
    key_flat = key_heads.reshape(row_total, kv_cols)
    value_flat = value_lin.astype(jnp.bfloat16)
    group_size = Q_HEADS // KV_HEADS
    start_state = (
        jnp.full((KV_HEADS, group_size, row_total), -1e30, jnp.float32),
        jnp.zeros((KV_HEADS, group_size, row_total), jnp.float32),
        jnp.zeros((KV_HEADS, group_size, row_total, HEAD), jnp.float32),
    )

    def strided_rank(slots_seen):
        return slots_seen // KEEP_DEV + slots_seen % KEEP_DEV * shard_count

    final_top, final_total, final_acc = make_fold(
        query_heads,
        query_ranks,
        strided_rank,
        start_state,
        (
            lax.all_gather(key_flat, "blk", axis=0, tiled=True),
            lax.all_gather(value_flat, "blk", axis=0, tiled=True),
        ),
    )
    attended = (
        (final_acc / final_total[..., None])
        .transpose(2, 0, 1, 3)
        .reshape(row_total, query_cols)
        .astype(jnp.bfloat16)
    )
    update = jnp.dot(attended, full_out, preferred_element_type=jnp.float32)
    update = update.astype(jnp.bfloat16)
    slot_grid = (
        jnp.arange(slot_count, dtype=jnp.int32)[:, None] * shard_count
        + jnp.mod(device - starts, shard_count)[None, :]
    )
    back_valid = slot_grid < all_counts[None, :]
    local_place = (starts[None, :] + slot_grid - device) // shard_count
    clipped = jnp.where(back_valid, local_place, 0)
    back_rows = jnp.where(back_valid[..., None], update[clipped], jnp.zeros((), jnp.bfloat16))
    returned = lax.all_to_all(back_rows, "blk", split_axis=1, concat_axis=1, tiled=True)
    returned = jnp.roll(returned, -own_start, axis=1).reshape(slot_count * shard_count, width)
    final = (
        token_rows.astype(jnp.float32) + gate_value[:, None] * returned.astype(jnp.float32)
    ).astype(jnp.bfloat16)
    target = jnp.where(is_valid, kept_idx[0], TOK_DEV)
    return hidden.at[target].set(final, mode="drop")


def solution(mesh):
    placed = (
        P(("groups", "blk"), None),
        P(("groups", "blk"), None),
        P(("groups", "blk")),
        P(),
        P(),
        P(),
        P("blk", None),
        P("blk", None),
        P("blk", None),
        P("blk", None),
    )
    return jax.shard_map(
        body, mesh=mesh, in_specs=placed, out_specs=P(("groups", "blk"), None), check_vma=False
    )
```

profile of v0, /device:TPU:0, one launch (start us, length us, event | category | flops | bytes accessed | tf_op | source)
XLA Modules:
  0.0 215.0 jit_solution(3244303445806012775)
XLA Ops:
  6.5 1.6 copy.93
  8.2 0.7 all-gather.6.cloned.1.call-update
  9.6 0.6 dynamic-slice
  10.2 0.7 dynamic-update-slice
  10.9 13.8 %all-reduce = s32[16]{0:T(128)S(1)} all-reduce(s32[16]{0:T(128)S(1)} %dynamic-update-slice), channel_id=1, replica_groups=mesh['groups'=2,'blk'=16] {'blk'}, use_global_device_ids=true, to_apply=%add | all-reduce | flops 16 | bytes 128
  24.9 0.1 reduce
  25.0 0.6 dynamic_slice.30
  27.6 0.6 dynamic_slice.29
  28.2 0.6 fusion.45
  28.9 0.9 gather_fusion
  29.8 0.6 add_compare_fusion
  30.4 0.3 copy_select_fusion.1
  30.8 1.0 fusion.30
  31.8 3.6 %all-to-all-start = ((bf16[8,16,2048]{2,0,1:T(8,128)(2,1)}), bf16[8,16,2048]{2,0,1:T(8,128)(2,1)S(1)}, u32[]{:S(2)}, u32[]{:S(2)}) async-start(bf16[8,16,2048]{2,0,1:T(8,128)(2,1)} %fusion.30), calls=%async_computation | async-start | bytes 1048576 | tf_op jit(solution)/shard_map/all_to_all | solution.py:102
  35.5 0.8 gather_fusion.1
  36.4 25.9 %all-gather = s32[16,1,128]{2,1,0:T(1,128)S(1)} all-gather(s32[1,1,128]{2,1,0:T(1,128)S(1)} %bitcast.125), channel_id=1, replica_groups=mesh['groups'=2,'blk'=16] {'blk'}, dimensions={0}, use_global_device_ids=true | all-gather | bytes 8704 | tf_op jit(solution)/shard_map/all_gather | solution.py:89
  62.3 0.8 gather_fusion.3
  63.3 0.2 multiply_cosine_fusion
  63.5 23.3 %all_gather.29 = bf16[2048,128]{1,0:T(8,128)(2,1)S(1)} all-gather(bf16[128,128]{1,0:T(8,128)(2,1)S(1)} %copy-done.3), channel_id=1, replica_groups=mesh['groups'=2,'blk'=16] {'blk'}, dimensions={0}, use_global_device_ids=true | all-gather | bytes 557056 | tf_op jit(solution)/shard_map/all_gather | solution.py:117
  86.8 19.3 %all_gather.25 = bf16[2048,128]{1,0:T(8,128)(2,1)S(1)} all-gather(bf16[128,128]{1,0:T(8,128)(2,1)S(1)} %copy-done.4), channel_id=1, replica_groups=mesh['groups'=2,'blk'=16] {'blk'}, dimensions={0}, use_global_device_ids=true | all-gather | bytes 557056 | tf_op jit(solution)/shard_map/all_gather | solution.py:116
  106.1 0.3 copy.56
  106.4 0.7 gather_fusion.2
  107.1 0.2 fusion.25
  107.3 0.3 fusion.53
  107.6 0.1 reshape.540
  107.7 0.1 multiply_reduce_fusion.1
  107.8 0.1 multiply_multiply_fusion.1
  108.0 0.2 subtract_convert_fusion.1
  108.2 0.1 pad_maximum_fusion.1
  108.4 0.3 convolution_convert_fusion.1
  108.7 20.5 %all_gather.30 = bf16[1024,128]{1,0:T(8,128)(2,1)S(1)} all-gather(bf16[64,128]{1,0:T(8,128)(2,1)S(1)} %convolution_convert_fusion.1), channel_id=1, replica_groups=mesh['groups'=2,'blk'=16] {'blk'}, dimensions={0}, use_global_device_ids=true | all-gather | bytes 278528 | tf_op jit(solution)/shard_map/all_gather | solution.py:152
  129.1 20.5 %all_gather.27 = bf16[1024,128]{1,0:T(8,128)(2,1)S(1)} all-gather(bf16[64,128]{1,0:T(8,128)(2,1)S(1)} %convert_element_type.65), channel_id=1, replica_groups=mesh['groups'=2,'blk'=16] {'blk'}, dimensions={0}, use_global_device_ids=true | all-gather | bytes 278528 | tf_op jit(solution)/shard_map/all_gather | solution.py:151
  149.6 5.0 %fusion.51 = f32[64,2048]{1,0:T(8,128)S(1)} fusion(bf16[2048,2048]{1,0:T(8,128)(2,1)} %all-gather.4.cloned.1.call-done, bf16[64,2048]{1,0:T(8,128)(2,1)S(1)} %gather_fusion.2, f32[2048]{0:T(1024)S(1)} %copy-done.2, f32[64]{0:T(128)S(1)} %add_rsqrt_fusion.2), kind=kOutput, calls=%fused_computation.132 | convolution fusion | flops 537395200 | bytes 9183488 | tf_op jit(solution)/shard_map/dot_general | solution.py:120
  154.6 0.4 reshape.541
  155.0 0.3 multiply_reduce_fusion
  155.4 0.3 multiply_multiply_fusion
  155.8 0.5 subtract_convert_fusion
  156.3 0.2 copy.59
  156.5 0.2 copy.60
  156.7 0.3 pad_maximum_fusion
  157.1 19.5 %while.20 = (s32[]{:T(128)}, f32[2,16,64]{2,1,0:T(8,128)S(1)}, f32[2,16,64]{2,1,0:T(8,128)S(1)}, f32[2,16,64,64]{3,2,1,0:T(8,128)S(1)}, bf16[1024,128]{1,0:T(8,1...) while((s32[]{:T(128)}, f32[2,16,64]{2,1,0:T(8,128)S(1)}, ...), condition=%wide.region_8.10_spmd.clone, body=%wide.region_5.9_spmd.clone.sunk | while | flops 282514560 | bytes 15471291 | solution.py:70
  157.1 0.1 copy.75
  157.3 2.7 %fusion.79 = (f32[2,16,64]{2,1,0:T(8,128)S(1)}, f32[2,512,64,16]{1,2,3,0:T(8,128)}) fusion(pred[64,512]{1,0:T(8,128)(4,1)S(1)} %broadcast_compare_fusion.2, bf16[512,2,64,1]{0,2,3,1:T(8,128)(2,1)S(1)} %bitcast.117, bf16[64,2,16,64]{3,0,2,1:T(8,128)(2,1)S(1)} %get-tuple-element.414), kind=kOutput, calls=%fused_computation.9.clone.1 | convolution fusion | flops 137361408 | bytes 4628480 | tf_op jit(solution)/shard_map/while/body/eval_jaxpr/agch,bgh->gcab/dot_general | solution.py:41
  160.0 3.4 %fusion.80 = f32[2,16,64]{2,1,0:T(8,128)S(1)} fusion(f32[2,512,64,16]{1,2,3,0:T(8,128)} %get-tuple-element.381, f32[2,16,64]{2,1,0:T(8,128)S(1)} %select_maximum_fusion.2, pred[64,512]{1,0:T(8,128)(4,1)S(1)} %broadcast_compare_fusion.2), kind=kLoop, calls=%fused_computation.11.clone.1 | loop fusion | flops 5240832 | bytes 4243456 | tf_op jit(solution)/shard_map/while/body/eval_jaxpr/reduce_sum | solution.py:49
  163.4 0.1 copy.76
  163.6 3.1 %fusion.82 = f32[2,16,64,64]{3,2,1,0:T(8,128)S(1)} fusion(bf16[512,2,64,1]{0,2,3,1:T(8,128)(2,1)S(1)} %bitcast.120, f32[2,512,64,16]{1,2,3,0:T(8,128)} %get-tuple-element.381, f32[2,16,64]{2,1,0:T(8,128)S(1)} %select_maximum_fusion.2, pred[64,512]{1,0:T(8,128)(4,1)S(1)} %broadcast_compare_fusion.2, f32[2,16,64,64]{3,2,1,0:T(8,128)S(1)} %get-tuple-element.400, ...), kind=kOutput, calls=%fused_computation.14.clone.1 | convolution fusion | flops 139853824 | bytes 5423105 | tf_op jit(solution)/shard_map/while/body/eval_jaxpr/gcab,bgh->gcah/dot_general | solution.py:50
  166.8 0.1 copy.75
  167.0 2.7 %fusion.79 = (f32[2,16,64]{2,1,0:T(8,128)S(1)}, f32[2,512,64,16]{1,2,3,0:T(8,128)}) fusion(pred[64,512]{1,0:T(8,128)(4,1)S(1)} %broadcast_compare_fusion.2, bf16[512,2,64,1]{0,2,3,1:T(8,128)(2,1)S(1)} %bitcast.117, bf16[64,2,16,64]{3,0,2,1:T(8,128)(2,1)S(1)} %get-tuple-element.414), kind=kOutput, calls=%fused_computation.9.clone.1 | convolution fusion | flops 137361408 | bytes 4628480 | tf_op jit(solution)/shard_map/while/body/eval_jaxpr/agch,bgh->gcab/dot_general | solution.py:41
  169.7 3.5 %fusion.80 = f32[2,16,64]{2,1,0:T(8,128)S(1)} fusion(f32[2,512,64,16]{1,2,3,0:T(8,128)} %get-tuple-element.381, f32[2,16,64]{2,1,0:T(8,128)S(1)} %select_maximum_fusion.2, pred[64,512]{1,0:T(8,128)(4,1)S(1)} %broadcast_compare_fusion.2), kind=kLoop, calls=%fused_computation.11.clone.1 | loop fusion | flops 5240832 | bytes 4243456 | tf_op jit(solution)/shard_map/while/body/eval_jaxpr/reduce_sum | solution.py:49
  173.3 0.1 copy.76
  173.4 3.1 %fusion.82 = f32[2,16,64,64]{3,2,1,0:T(8,128)S(1)} fusion(bf16[512,2,64,1]{0,2,3,1:T(8,128)(2,1)S(1)} %bitcast.120, f32[2,512,64,16]{1,2,3,0:T(8,128)} %get-tuple-element.381, f32[2,16,64]{2,1,0:T(8,128)S(1)} %select_maximum_fusion.2, pred[64,512]{1,0:T(8,128)(4,1)S(1)} %broadcast_compare_fusion.2, f32[2,16,64,64]{3,2,1,0:T(8,128)S(1)} %get-tuple-element.400, ...), kind=kOutput, calls=%fused_computation.14.clone.1 | convolution fusion | flops 139853824 | bytes 5423105 | tf_op jit(solution)/shard_map/while/body/eval_jaxpr/gcab,bgh->gcah/dot_general | solution.py:50
  176.5 0.3 fusion.31
  176.9 0.3 copy.63
  177.2 0.5 convert_element_type.69
  177.7 5.0 %convolution_convert_fusion = bf16[64,2048]{1,0:T(8,128)(2,1)S(1)} fusion(bf16[64,2048]{1,0:T(8,128)(2,1)S(1)} %convert_element_type.69, bf16[2048,2048]{1,0:T(8,128)(2,1)} %all-gather.6.cloned.1.call-done), kind=kOutput, calls=%fused_computation.38 | convolution fusion | flops 537001984 | bytes 8912896 | tf_op jit(solution)/shard_map/dot_general | solution.py:161
  182.7 0.9 gather_fusion.4
  183.6 1.1 copy_select_fusion
  184.7 3.8 %all-to-all-start.1 = ((bf16[8,16,2048]{2,0,1:T(8,128)(2,1)}), bf16[8,16,2048]{2,0,1:T(8,128)(2,1)S(1)}, u32[]{:S(2)}, u32[]{:S(2)}) async-start(bf16[8,16,2048]{2,0,1:T(8,128)(2,1)} %copy_select_fusion), calls=%async_computation.1 | async-start | bytes 1048576 | tf_op jit(solution)/shard_map/all_to_all | solution.py:171
  189.2 0.2 fusion.22
  189.4 13.1 %all-to-all-done.1 = bf16[8,16,2048]{2,0,1:T(8,128)(2,1)S(1)} async-done(((bf16[8,16,2048]{2,0,1:T(8,128)(2,1)}), bf16[8,16,2048]{2,0,1:T(8,128)(2,1)S(1)}, u32[]{:S(2)}, u32[]{:S(2)}) %all-to-all-start.1) | async-done | bytes 524320 | tf_op jit(solution)/shard_map/all_to_all | solution.py:171
  202.5 0.2 fusion.29
  202.8 0.6 copy.65
  203.4 0.2 fusion.24
  203.6 4.6 %scatter_fusion = bf16[512,2048]{1,0:T(8,128)(2,1)} fusion(bf16[512,2048]{1,0:T(8,128)(2,1)} %copy-done, s32[128]{0:T(128)S(1)} %get-tuple-element.323, bf16[128,2048]{1,0:T(8,128)(2,1)S(1)} %fusion.24), kind=kCustom, calls=%fused_computation.5 | custom fusion | bytes 1573376 | tf_op jit(solution)/shard_map/scatter | solution.py:177
  (65 shorter events, 1.1 us)
Async XLA Ops:
  6.5 3.1 %copy-start.8 = (u32[32]{0:T(128)S(1)}, u32[32]{0:T(128)}, u32[]{:S(2)}) copy-start(u32[32]{0:T(128)} %constant.259) | copy-start | bytes 388
  6.5 21.7 %copy-start.6 = (s32[1,128]{1,0:T(1,128)S(1)}, s32[1,128]{1,0:T(1,128)}, u32[]{:S(2)}) copy-start(s32[1,128]{1,0:T(1,128)} %param.15) | copy-start | bytes 1540
  6.5 143.1 %all-gather.4.cloned.1.call-start = ((), (), s32[]{:S(2)}) async-start(), calls=%async_computation.2 | async-start | bytes 8912896 | tf_op jit(solution)/shard_map/all_gather | solution.py:115
  8.2 23.6 %copy-start = (bf16[512,2048]{1,0:T(8,128)(2,1)}, bf16[512,2048]{1,0:T(8,128)(2,1)S(1)}, u32[]{:S(2)}) copy-start(bf16[512,2048]{1,0:T(8,128)(2,1)S(1)} %copy.93) | copy-start | bytes 6291460
  8.2 169.5 %all-gather.6.cloned.1.call-start = ((), (), s32[]{:S(2)}) async-start(), calls=%async_computation.3 | async-start | bytes 8912896 | tf_op jit(solution)/shard_map/all_gather | solution.py:118
  28.8 34.3 %copy-start.7 = (f32[2,64]{1,0:T(2,128)S(1)}, f32[2,64]{1,0:T(2,128)}, u32[]{:S(2)}) copy-start(f32[2,64]{1,0:T(2,128)} %param.19) | copy-start | bytes 1540
  28.8 34.7 %copy-start.3 = (bf16[128,128]{1,0:T(8,128)(2,1)S(1)}, bf16[128,128]{1,0:T(8,128)(2,1)}, u32[]{:S(2)}) copy-start(bf16[128,128]{1,0:T(8,128)(2,1)} %param.22) | copy-start | bytes 98308
  28.9 57.9 %copy-start.4 = (bf16[128,128]{1,0:T(8,128)(2,1)S(1)}, bf16[128,128]{1,0:T(8,128)(2,1)}, u32[]{:S(2)}) copy-start(bf16[128,128]{1,0:T(8,128)(2,1)} %param.21) | copy-start | bytes 98308
  30.8 76.5 %copy-start.2 = (f32[2048]{0:T(1024)S(1)}, f32[2048]{0:T(1024)}, u32[]{:S(2)}) copy-start(f32[2048]{0:T(1024)} %param.18) | copy-start | bytes 24580
  31.8 74.3 %all-to-all-start = ((bf16[8,16,2048]{2,0,1:T(8,128)(2,1)}), bf16[8,16,2048]{2,0,1:T(8,128)(2,1)S(1)}, u32[]{:S(2)}, u32[]{:S(2)}) async-start(bf16[8,16,2048]{2,0,1:T(8,128)(2,1)} %fusion.30), calls=%async_computation | async-start | bytes 1048576 | tf_op jit(solution)/shard_map/all_to_all | solution.py:102
  155.4 1.6 copy-start.1
  182.7 6.5 %copy-start.5 = (bf16[2048]{0:T(1024)(128)(2,1)S(1)}, bf16[2048]{0:T(1024)(128)(2,1)}, u32[]{:S(2)}) copy-start(bf16[2048]{0:T(1024)(128)(2,1)} %param.17) | copy-start | bytes 12292
  184.7 17.8 %all-to-all-start.1 = ((bf16[8,16,2048]{2,0,1:T(8,128)(2,1)}), bf16[8,16,2048]{2,0,1:T(8,128)(2,1)S(1)}, u32[]{:S(2)}, u32[]{:S(2)}) async-start(bf16[8,16,2048]{2,0,1:T(8,128)(2,1)} %copy_select_fusion), calls=%async_computation.1 | async-start | bytes 1048576 | tf_op jit(solution)/shard_map/all_to_all | solution.py:171
Sparse Core Ops, SparseCore 0:
  9.5 84.1 all-gather.3
  95.8 77.4 all-gather.5
where the time goes:
time: 216 us; the launch traced here: 215 us
  blocking collectives  123 us (57%)
  matrix products  22.3 us (10%)
  between operations  17 us (8%)
  local copies, waits for them, and re-layouts  16.5 us (8%)
  other arithmetic  14.6 us (7%)
  waiting for transfers between devices  13.8 us (6%)
  starting transfers between devices  7.41 us (3%)
    all_gather x1, blocking collectives, body(): lax.all_gather(kept_idx, 'blk', axis=0, tiled=True)  25.9 us
    all_gather x1, blocking collectives, body(): lax.all_gather(value_weight, 'blk', axis=0, tiled=True)  23.3 us
    all_gather x1, blocking collectives, body(): lax.all_gather(value_flat, 'blk', axis=0, tiled=True)  20.5 us
    all_gather x1, blocking collectives, body(): lax.all_gather(key_flat, 'blk', axis=0, tiled=True)  20.5 us
    all_gather x1, blocking collectives, body(): lax.all_gather(key_weight, 'blk', axis=0, tiled=True)  19.3 us
    unnamed x1, blocking collectives  13.8 us
    all_to_all x1, waiting for transfers between devices, body(): lax.all_to_all(back_rows, 'blk', split_axis=1, concat_axis=1, tiled=True)  13.1 us
    reduce_sum x2, other arithmetic, attend(): new_total = prev_total * factor + jnp.sum(weights, axis=-1)  6.96 us
  transfers between devices with their start and end apart: 4, of which 1 were waited for; matrix products, arithmetic and copies ran while one was open for 18% of the time, Pallas kernels for 0%

commit v1 on v0

--- a/solution.py
+++ b/solution.py
@@ -168,7 +168,15 @@
     local_place = (starts[None, :] + slot_grid - device) // shard_count
     clipped = jnp.where(back_valid, local_place, 0)
     back_rows = jnp.where(back_valid[..., None], update[clipped], jnp.zeros((), jnp.bfloat16))
-    returned = lax.all_to_all(back_rows, "blk", split_axis=1, concat_axis=1, tiled=True)
+    returned = jnp.concatenate(
+        lax.all_to_all(
+            jnp.stack(jnp.split(back_rows, lax.axis_size("blk"), axis=1)),
+            axis_name="blk",
+            split_axis=0,
+            concat_axis=0,
+        ),
+        axis=1,
+    )
     returned = jnp.roll(returned, -own_start, axis=1).reshape(slot_count * shard_count, width)
     final = (
         token_rows.astype(jnp.float32) + gate_value[:, None] * returned.astype(jnp.float32)

time: 216 us -> 225 us (1.042)
  local copies, waits for them, and re-layouts: 16.5 us -> 26.2 us
    unnamed x23 -> x38, local copies, waits for them, and re-layouts: 3.01 us -> 12.1 us
  transfers between devices with their start and end apart: 4 -> 4, of which waited for: 1 -> 1; matrix products, arithmetic and copies ran while one was open for 18% -> 17% of each run, Pallas kernels for 0% -> 0%
where the time goes in v1:
time: 225 us; the launch traced here: 224 us
  blocking collectives  123 us (55%)
  local copies, waits for them, and re-layouts  26.2 us (12%)
  matrix products  22.3 us (10%)
  between operations  17 us (8%)
  waiting for transfers between devices  13.8 us (6%)
  other arithmetic  13.8 us (6%)
  starting transfers between devices  7.41 us (3%)
    all_gather x1, blocking collectives, body(): lax.all_gather(kept_idx, 'blk', axis=0, tiled=True)  25.9 us
    all_gather x1, blocking collectives, body(): lax.all_gather(value_weight, 'blk', axis=0, tiled=True)  23.3 us
    all_gather x1, blocking collectives, body(): lax.all_gather(value_flat, 'blk', axis=0, tiled=True)  20.5 us
    all_gather x1, blocking collectives, body(): lax.all_gather(key_flat, 'blk', axis=0, tiled=True)  20.5 us
    all_gather x1, blocking collectives, body(): lax.all_gather(key_weight, 'blk', axis=0, tiled=True)  19.3 us
    unnamed x1, blocking collectives  13.8 us
    all_to_all x1, waiting for transfers between devices, body(): lax.all_to_all(jnp.stack(jnp.split(back_rows, lax.axis_size('blk'), axis=...  13.1 us
    unnamed x38, local copies, waits for them, and re-layouts  12.1 us
  transfers between devices with their start and end apart: 4, of which 1 were waited for; matrix products, arithmetic and copies ran while one was open for 17% of the time, Pallas kernels for 0%

profile of v1, /device:TPU:0, one launch (start us, length us, event | category | flops | bytes accessed | tf_op | source)
XLA Modules:
  0.0 223.9 jit_solution(33316900938429207)
XLA Ops:
  6.5 1.6 copy.130
  8.2 0.7 all-gather.6.cloned.1.call-update
  9.6 0.6 dynamic-slice
  10.2 0.7 dynamic-update-slice
  10.9 13.8 %all-reduce = s32[16]{0:T(128)S(1)} all-reduce(s32[16]{0:T(128)S(1)} %dynamic-update-slice), channel_id=1, replica_groups=mesh['groups'=2,'blk'=16] {'blk'}, use_global_device_ids=true, to_apply=%add | all-reduce | flops 16 | bytes 128
  25.0 0.6 dynamic_slice.30
  27.6 0.6 dynamic_slice.29
  28.2 0.6 fusion.61
  28.9 0.9 gather_fusion
  29.8 0.6 add_compare_fusion
  30.4 0.3 copy_select_fusion.1
  30.8 1.0 fusion.30
  31.8 3.6 %all-to-all-start = ((bf16[8,16,2048]{2,0,1:T(8,128)(2,1)}), bf16[8,16,2048]{2,0,1:T(8,128)(2,1)S(1)}, u32[]{:S(2)}, u32[]{:S(2)}) async-start(bf16[8,16,2048]{2,0,1:T(8,128)(2,1)} %fusion.30), calls=%async_computation | async-start | bytes 1048576 | tf_op jit(solution)/shard_map/all_to_all | solution.py:102
  35.5 0.8 gather_fusion.1
  36.4 25.9 %all-gather = s32[16,1,128]{2,1,0:T(1,128)S(1)} all-gather(s32[1,1,128]{2,1,0:T(1,128)S(1)} %bitcast.193), channel_id=1, replica_groups=mesh['groups'=2,'blk'=16] {'blk'}, dimensions={0}, use_global_device_ids=true | all-gather | bytes 8704 | tf_op jit(solution)/shard_map/all_gather | solution.py:89
  62.3 0.8 gather_fusion.3
  63.5 23.3 %all_gather.29 = bf16[2048,128]{1,0:T(8,128)(2,1)S(1)} all-gather(bf16[128,128]{1,0:T(8,128)(2,1)S(1)} %copy-done.3), channel_id=1, replica_groups=mesh['groups'=2,'blk'=16] {'blk'}, dimensions={0}, use_global_device_ids=true | all-gather | bytes 557056 | tf_op jit(solution)/shard_map/all_gather | solution.py:117
  86.8 19.3 %all_gather.25 = bf16[2048,128]{1,0:T(8,128)(2,1)S(1)} all-gather(bf16[128,128]{1,0:T(8,128)(2,1)S(1)} %copy-done.4), channel_id=1, replica_groups=mesh['groups'=2,'blk'=16] {'blk'}, dimensions={0}, use_global_device_ids=true | all-gather | bytes 557056 | tf_op jit(solution)/shard_map/all_gather | solution.py:116
  106.1 0.3 copy.78
  106.4 0.7 gather_fusion.2
  107.3 0.3 fusion.69
  108.4 0.3 convolution_convert_fusion.1
  108.7 20.5 %all_gather.30 = bf16[1024,128]{1,0:T(8,128)(2,1)S(1)} all-gather(bf16[64,128]{1,0:T(8,128)(2,1)S(1)} %convolution_convert_fusion.1), channel_id=1, replica_groups=mesh['groups'=2,'blk'=16] {'blk'}, dimensions={0}, use_global_device_ids=true | all-gather | bytes 278528 | tf_op jit(solution)/shard_map/all_gather | solution.py:152
  129.1 20.5 %all_gather.27 = bf16[1024,128]{1,0:T(8,128)(2,1)S(1)} all-gather(bf16[64,128]{1,0:T(8,128)(2,1)S(1)} %convert_element_type.65), channel_id=1, replica_groups=mesh['groups'=2,'blk'=16] {'blk'}, dimensions={0}, use_global_device_ids=true | all-gather | bytes 278528 | tf_op jit(solution)/shard_map/all_gather | solution.py:151
  149.6 5.0 %fusion.67 = f32[64,2048]{1,0:T(8,128)S(1)} fusion(bf16[2048,2048]{1,0:T(8,128)(2,1)} %all-gather.4.cloned.1.call-done, bf16[64,2048]{1,0:T(8,128)(2,1)S(1)} %gather_fusion.2, f32[2048]{0:T(1024)S(1)} %copy-done.2, f32[64]{0:T(128)S(1)} %add_rsqrt_fusion.2), kind=kOutput, calls=%fused_computation.164 | convolution fusion | flops 537395200 | bytes 9183488 | tf_op jit(solution)/shard_map/dot_general | solution.py:120
  154.6 0.4 reshape.547
  155.0 0.3 multiply_reduce_fusion
  155.4 0.3 multiply_multiply_fusion
  155.8 0.5 subtract_convert_fusion
  156.7 0.3 pad_maximum_fusion
  157.1 19.5 %while.20 = (s32[]{:T(128)}, f32[2,16,64]{2,1,0:T(8,128)S(1)}, f32[2,16,64]{2,1,0:T(8,128)S(1)}, f32[2,16,64,64]{3,2,1,0:T(8,128)S(1)}, bf16[1024,128]{1,0:T(8,1...) while((s32[]{:T(128)}, f32[2,16,64]{2,1,0:T(8,128)S(1)}, ...), condition=%wide.region_8.10_spmd.clone, body=%wide.region_5.9_spmd.clone.sunk | while | flops 282514560 | bytes 15471291 | solution.py:70
  157.3 2.7 %fusion.95 = (f32[2,16,64]{2,1,0:T(8,128)S(1)}, f32[2,512,64,16]{1,2,3,0:T(8,128)}) fusion(pred[64,512]{1,0:T(8,128)(4,1)S(1)} %broadcast_compare_fusion.2, bf16[512,2,64,1]{0,2,3,1:T(8,128)(2,1)S(1)} %bitcast.184, bf16[64,2,16,64]{3,0,2,1:T(8,128)(2,1)S(1)} %get-tuple-element.414), kind=kOutput, calls=%fused_computation.9.clone.1 | convolution fusion | flops 137361408 | bytes 4628480 | tf_op jit(solution)/shard_map/while/body/eval_jaxpr/agch,bgh->gcab/dot_general | solution.py:41
  160.0 3.4 %fusion.96 = f32[2,16,64]{2,1,0:T(8,128)S(1)} fusion(f32[2,512,64,16]{1,2,3,0:T(8,128)} %get-tuple-element.381, f32[2,16,64]{2,1,0:T(8,128)S(1)} %select_maximum_fusion.2, pred[64,512]{1,0:T(8,128)(4,1)S(1)} %broadcast_compare_fusion.2), kind=kLoop, calls=%fused_computation.11.clone.1 | loop fusion | flops 5240832 | bytes 4243456 | tf_op jit(solution)/shard_map/while/body/eval_jaxpr/reduce_sum | solution.py:49
  163.6 3.1 %fusion.98 = f32[2,16,64,64]{3,2,1,0:T(8,128)S(1)} fusion(bf16[512,2,64,1]{0,2,3,1:T(8,128)(2,1)S(1)} %bitcast.187, f32[2,512,64,16]{1,2,3,0:T(8,128)} %get-tuple-element.381, f32[2,16,64]{2,1,0:T(8,128)S(1)} %select_maximum_fusion.2, pred[64,512]{1,0:T(8,128)(4,1)S(1)} %broadcast_compare_fusion.2, f32[2,16,64,64]{3,2,1,0:T(8,128)S(1)} %get-tuple-element.400, ...), kind=kOutput, calls=%fused_computation.14.clone.1 | convolution fusion | flops 139853824 | bytes 5423105 | tf_op jit(solution)/shard_map/while/body/eval_jaxpr/gcab,bgh->gcah/dot_general | solution.py:50
  167.0 2.7 %fusion.95 = (f32[2,16,64]{2,1,0:T(8,128)S(1)}, f32[2,512,64,16]{1,2,3,0:T(8,128)}) fusion(pred[64,512]{1,0:T(8,128)(4,1)S(1)} %broadcast_compare_fusion.2, bf16[512,2,64,1]{0,2,3,1:T(8,128)(2,1)S(1)} %bitcast.184, bf16[64,2,16,64]{3,0,2,1:T(8,128)(2,1)S(1)} %get-tuple-element.414), kind=kOutput, calls=%fused_computation.9.clone.1 | convolution fusion | flops 137361408 | bytes 4628480 | tf_op jit(solution)/shard_map/while/body/eval_jaxpr/agch,bgh->gcab/dot_general | solution.py:41
  169.7 3.5 %fusion.96 = f32[2,16,64]{2,1,0:T(8,128)S(1)} fusion(f32[2,512,64,16]{1,2,3,0:T(8,128)} %get-tuple-element.381, f32[2,16,64]{2,1,0:T(8,128)S(1)} %select_maximum_fusion.2, pred[64,512]{1,0:T(8,128)(4,1)S(1)} %broadcast_compare_fusion.2), kind=kLoop, calls=%fused_computation.11.clone.1 | loop fusion | flops 5240832 | bytes 4243456 | tf_op jit(solution)/shard_map/while/body/eval_jaxpr/reduce_sum | solution.py:49
  173.4 3.1 %fusion.98 = f32[2,16,64,64]{3,2,1,0:T(8,128)S(1)} fusion(bf16[512,2,64,1]{0,2,3,1:T(8,128)(2,1)S(1)} %bitcast.187, f32[2,512,64,16]{1,2,3,0:T(8,128)} %get-tuple-element.381, f32[2,16,64]{2,1,0:T(8,128)S(1)} %select_maximum_fusion.2, pred[64,512]{1,0:T(8,128)(4,1)S(1)} %broadcast_compare_fusion.2, f32[2,16,64,64]{3,2,1,0:T(8,128)S(1)} %get-tuple-element.400, ...), kind=kOutput, calls=%fused_computation.14.clone.1 | convolution fusion | flops 139853824 | bytes 5423105 | tf_op jit(solution)/shard_map/while/body/eval_jaxpr/gcab,bgh->gcah/dot_general | solution.py:50
  176.5 0.3 fusion.31
  176.9 0.3 copy.85
  177.2 0.5 convert_element_type.69
  177.7 5.0 %convolution_convert_fusion = bf16[64,2048]{1,0:T(8,128)(2,1)S(1)} fusion(bf16[64,2048]{1,0:T(8,128)(2,1)S(1)} %convert_element_type.69, bf16[2048,2048]{1,0:T(8,128)(2,1)} %all-gather.6.cloned.1.call-done), kind=kOutput, calls=%fused_computation.38 | convolution fusion | flops 537001984 | bytes 8912896 | tf_op jit(solution)/shard_map/dot_general | solution.py:161
  182.7 0.9 gather_fusion.4
  183.6 0.3 copy_select_fusion
  183.9 0.6 fusion.47
  184.5 0.6 fusion.46
  185.1 0.6 fusion.45
  185.7 0.6 fusion.44
  186.3 0.6 fusion.43
  187.0 0.6 fusion.42
  187.6 0.6 fusion.41
  188.2 0.6 fusion.40
  188.8 0.6 fusion.39
  189.4 0.6 fusion.38
  190.0 0.6 fusion.37
  190.6 0.6 fusion.36
  191.2 0.6 fusion.35
  191.8 0.6 fusion.34
  192.4 0.6 fusion.33
  193.0 0.6 fusion.32
  193.6 3.8 %all-to-all-start.1 = ((bf16[16,8,1,2048]{3,1,2,0:T(8,128)(2,1)}), bf16[16,8,1,2048]{3,1,2,0:T(8,128)(2,1)S(1)}, u32[]{:S(2)}, u32[]{:S(2)}) async-start(bf16[16,8,1,2048]{3,1,2,0:T(8,128)(2,1)} %fusion.32), calls=%async_computation.1 | async-start | bytes 1048576 | tf_op jit(solution)/shard_map/all_to_all | solution.py:172
  198.1 0.2 fusion.22
  198.3 13.1 %all-to-all-done.1 = bf16[16,8,1,2048]{3,1,2,0:T(8,128)(2,1)S(1)} async-done(((bf16[16,8,1,2048]{3,1,2,0:T(8,128)(2,1)}), bf16[16,8,1,2048]{3,1,2,0:T(8,128)(2,1)S(1)}, u32[]{:S(2)}, u32[]{:S(2)}) %all-to-all-start.1) | async-done | bytes 524320 | tf_op jit(solution)/shard_map/all_to_all | solution.py:172
  211.7 0.6 copy.87
  212.5 4.6 %scatter_fusion = bf16[512,2048]{1,0:T(8,128)(2,1)} fusion(bf16[512,2048]{1,0:T(8,128)(2,1)} %copy-done, s32[128]{0:T(128)S(1)} %get-tuple-element.323, bf16[128,2048]{1,0:T(8,128)(2,1)S(1)} %fusion.24), kind=kCustom, calls=%fused_computation.5 | custom fusion | bytes 1573376 | tf_op jit(solution)/shard_map/scatter | solution.py:185
  (81 shorter events, 3.5 us)
Async XLA Ops:
  6.5 3.1 %copy-start.8 = (u32[32]{0:T(128)S(1)}, u32[32]{0:T(128)}, u32[]{:S(2)}) copy-start(u32[32]{0:T(128)} %constant.259) | copy-start | bytes 388
  6.5 21.7 %copy-start.6 = (s32[1,128]{1,0:T(1,128)S(1)}, s32[1,128]{1,0:T(1,128)}, u32[]{:S(2)}) copy-start(s32[1,128]{1,0:T(1,128)} %param.15) | copy-start | bytes 1540
  6.5 143.1 %all-gather.4.cloned.1.call-start = ((), (), s32[]{:S(2)}) async-start(), calls=%async_computation.2 | async-start | bytes 8912896 | tf_op jit(solution)/shard_map/all_gather | solution.py:115
  8.2 23.6 %copy-start = (bf16[512,2048]{1,0:T(8,128)(2,1)}, bf16[512,2048]{1,0:T(8,128)(2,1)S(1)}, u32[]{:S(2)}) copy-start(bf16[512,2048]{1,0:T(8,128)(2,1)S(1)} %copy.130) | copy-start | bytes 6291460
  8.2 169.5 %all-gather.6.cloned.1.call-start = ((), (), s32[]{:S(2)}) async-start(), calls=%async_computation.3 | async-start | bytes 8912896 | tf_op jit(solution)/shard_map/all_gather | solution.py:118
  28.8 34.3 %copy-start.7 = (f32[2,64]{1,0:T(2,128)S(1)}, f32[2,64]{1,0:T(2,128)}, u32[]{:S(2)}) copy-start(f32[2,64]{1,0:T(2,128)} %param.19) | copy-start | bytes 1540
  28.8 34.7 %copy-start.3 = (bf16[128,128]{1,0:T(8,128)(2,1)S(1)}, bf16[128,128]{1,0:T(8,128)(2,1)}, u32[]{:S(2)}) copy-start(bf16[128,128]{1,0:T(8,128)(2,1)} %param.22) | copy-start | bytes 98308
  28.9 57.9 %copy-start.4 = (bf16[128,128]{1,0:T(8,128)(2,1)S(1)}, bf16[128,128]{1,0:T(8,128)(2,1)}, u32[]{:S(2)}) copy-start(bf16[128,128]{1,0:T(8,128)(2,1)} %param.21) | copy-start | bytes 98308
  30.8 76.5 %copy-start.2 = (f32[2048]{0:T(1024)S(1)}, f32[2048]{0:T(1024)}, u32[]{:S(2)}) copy-start(f32[2048]{0:T(1024)} %param.18) | copy-start | bytes 24580
  31.8 74.3 %all-to-all-start = ((bf16[8,16,2048]{2,0,1:T(8,128)(2,1)}), bf16[8,16,2048]{2,0,1:T(8,128)(2,1)S(1)}, u32[]{:S(2)}, u32[]{:S(2)}) async-start(bf16[8,16,2048]{2,0,1:T(8,128)(2,1)} %fusion.30), calls=%async_computation | async-start | bytes 1048576 | tf_op jit(solution)/shard_map/all_to_all | solution.py:102
  155.4 1.6 copy-start.1
  182.7 15.4 %copy-start.5 = (bf16[2048]{0:T(1024)(128)(2,1)S(1)}, bf16[2048]{0:T(1024)(128)(2,1)}, u32[]{:S(2)}) copy-start(bf16[2048]{0:T(1024)(128)(2,1)} %param.17) | copy-start | bytes 12292
  193.6 17.8 %all-to-all-start.1 = ((bf16[16,8,1,2048]{3,1,2,0:T(8,128)(2,1)}), bf16[16,8,1,2048]{3,1,2,0:T(8,128)(2,1)S(1)}, u32[]{:S(2)}, u32[]{:S(2)}) async-start(bf16[16,8,1,2048]{3,1,2,0:T(8,128)(2,1)} %fusion.32), calls=%async_computation.1 | async-start | bytes 1048576 | tf_op jit(solution)/shard_map/all_to_all | solution.py:172
Sparse Core Ops, SparseCore 0:
  9.5 84.1 all-gather.3
  95.8 77.4 all-gather.5
